TPU v7x, 1024 devices: a whole 4x8x16 slice. The times are simulated.
1024 devices in a mesh: row: 64 (over y, x, core), col: 16 (over z).
Axes of the slice: x: 4, y: 8, z: 16, core: 2. Of those that a mesh axis runs over, the one named last changes fastest.
Arguments:
- weight: bfloat16 [8192, 24576], P('row', 'col'), may hold values from -6 to 6
- gradient: bfloat16 [8192, 24576], P('row', 'col'), may hold values from -80 to 80
- momentum: float32 [8192, 24576], P('row', 'col'), may hold values from -6 to 6
- old_basis: bfloat16 [256, 24576], P(None, 'col'), may hold values from -6 to 6
Outputs:
- new_weight: bfloat16 [8192, 24576], P('row', 'col')
- new_momentum: float32 [8192, 24576], P('row', 'col')
- new_basis: bfloat16 [256, 24576], P(None, 'col')
All inputs are finite; a program needn't handle non-finite values.
Results may differ from a plain program's by a relative error of at most 0.0056.
Values may be sent and summed in bfloat16 or wider, within the bound.
A program may use at most 32 MiB of HBM per device.

v0:
```python
import math

import jax
import jax.numpy as jnp
from jax import lax
from jax.sharding import Mesh
from jax.sharding import PartitionSpec as P

D = 8192
FF = 24576
RANK = 256
ROW = ("row_0", "row_1", "row_2")


epsilon = 1e-06
momentum_decay = 0.6
step_rate = 0.5


def sent_to_all(shard, axis):
    copies = jnp.broadcast_to(shard, (lax.axis_size(axis), *shard.shape))
    return lax.all_to_all(copies, axis, split_axis=0, concat_axis=0, tiled=True)


def over_copies(shard, axis):
    everything = sent_to_all(shard, axis)
    return jnp.sum(everything, axis=0)


def rows_for(lines, devices):
    spare = -lines.shape[0] % devices
    if not spare:
        return lines
    return jnp.concatenate([lines, jnp.zeros((spare, *lines.shape[1:]), lines.dtype)])


def own_block(blocks, axes, sequence):
    lengths = [lax.axis_size(a) for a in axes]
    blocks = blocks.reshape(*lengths, *blocks.shape[1:])
    blocks = blocks.transpose(*sequence, *range(len(axes), blocks.ndim))
    blocks = blocks.reshape(-1, *blocks.shape[len(axes) :])
    for k in sequence:
        blocks = lax.psum_scatter(blocks, axes[k], scatter_dimension=0, tiled=True)
    return blocks[0]


def all_blocks(shard, axes, sequence):
    blocks = shard
    for k in sequence:
        blocks = lax.all_gather(blocks, axes[k])
    done = sequence[::-1]
    back = [done.index(k) for k in range(len(axes))]
    blocks = blocks.transpose(*back, *range(len(axes), blocks.ndim))
    return blocks.reshape(-1, *shard.shape)


def total_of(shard, axes, sequence):
    devices, lines = (lax.axis_size(axes), shard.reshape(-1, *shard.shape[1:][-1:]))
    blocks = rows_for(lines, devices).reshape(devices, -1, *lines.shape[1:])
    own = own_block(blocks, axes, sequence)
    whole = all_blocks(own, axes, sequence[::-1]).reshape(-1, *lines.shape[1:])
    return whole[: len(lines)].reshape(shard.shape)


def cut_along(shard, dim, devices):
    lengths = shard.shape
    blocks = shard.reshape(*lengths[:dim], devices, lengths[dim] // devices, *lengths[dim + 1 :])
    return jnp.moveaxis(blocks, dim, 0)


def sum_at_owner(shard, axis, dim):
    blocks = cut_along(shard, dim, lax.axis_size(axis))
    arrived = lax.all_to_all(blocks, axis, split_axis=0, concat_axis=0, tiled=True)
    return arrived.sum(axis=0)


def joined_along(blocks, dim):
    lengths = list(blocks.shape[1:])
    lengths[dim] *= blocks.shape[0]
    return jnp.moveaxis(blocks, 0, dim).reshape(lengths)


def collect(shard, axis, dim):
    return joined_along(sent_to_all(shard, axis), dim)


def orthonormalize(left_rows, gram_matrix):
    chol_factor = jnp.linalg.cholesky(gram_matrix)
    return lax.linalg.triangular_solve(
        chol_factor, left_rows, left_side=False, lower=True, transpose_a=True
    ).astype(jnp.bfloat16)


def gram_of(left_rows):
    return lax.dot_general(
        left_rows,
        left_rows,
        (((0,), (0,)), ((), ())),
        precision=lax.Precision.HIGHEST,
        preferred_element_type=jnp.float32,
    )


def per_device(weight, gradient, momentum, old_basis):
    buffer = momentum + gradient.astype(jnp.float32)
    buffer_low = buffer.astype(jnp.bfloat16)
    local_left = lax.dot_general(
        buffer_low, old_basis, (((1,), (1,)), ((), ())), preferred_element_type=jnp.float32
    )
    left_factor = over_copies(local_left, "col")
    gram_matrix = total_of(gram_of(left_factor), ROW, (1, 2, 0))
    orthonormal = orthonormalize(left_factor, gram_matrix)
    right_share = sum_at_owner(
        lax.dot_general(
            orthonormal, buffer_low, (((0,), (0,)), ((), ())), preferred_element_type=jnp.float32
        ),
        ROW,
        0,
    )
    sum_squares = over_copies(jnp.sum(right_share * right_share, axis=1), "col")
    scale_share = jnp.sqrt(sum_squares / FF + epsilon)
    basis_share = (right_share / scale_share[:, None]).astype(jnp.bfloat16)
    new_basis = collect(basis_share, ROW, 0)
    col_scale = collect(scale_share, ROW, 0)
    scaled = (orthonormal.astype(jnp.float32) * col_scale[None, :]).astype(jnp.bfloat16)
    correction = jnp.dot(scaled, new_basis, preferred_element_type=jnp.float32)
    change = jnp.dot(orthonormal, new_basis, preferred_element_type=jnp.float32)
    new_momentum = buffer - (1.0 - momentum_decay) * correction
    factor = step_rate * math.sqrt(D / RANK)
    new_weight = (weight.astype(jnp.float32) - factor * change).astype(jnp.bfloat16)
    return (new_weight, new_momentum, new_basis)


def solution(mesh):
    finer = Mesh(
        mesh.devices.reshape(8, 4, 2, mesh.shape["col"]), ("row_0", "row_1", "row_2", "col")
    )
    return jax.shard_map(
        per_device,
        mesh=finer,
        in_specs=(P(ROW, "col"), P(ROW, "col"), P(ROW, "col"), P(None, "col")),
        out_specs=(P(ROW, "col"), P(ROW, "col"), P(None, "col")),
        check_vma=False,
    )
```

profile of v0, /device:TPU:1, one launch (start us, length us, event | category | flops | bytes accessed | tf_op | source)
XLA Modules:
  0.0 444.1 jit_solution(5191932213594163984)
XLA Ops:
  8.3 1.6 fusion.19
  10.1 109.6 %all_to_all.27 = f32[16,128,256]{2,1,0:T(8,128)S(1)} all-to-all(f32[16,128,256]{2,1,0:T(8,128)S(1)} %broadcast_in_dim.15), channel_id=1, replica_groups=mesh['row_0'=8,'row_1'=4,'row_2'=2,'col'=16] {'col'}, dimensions={0} | all-to-all | bytes 4194304 | tf_op jit(solution)/shard_map/all_to_all | solution.py:22
  121.2 31.2 %reduce-scatter.3.cloned.1.call-done = f32[16,4,256]{2,0,1:T(8,128)} async-done(((f32[64,4,256]{2,0,1:T(8,128)}), f32[16,4,256]{2,0,1:T(8,128)}) %reduce-scatter.3.cloned.1.call-update) | async-done | bytes 65552 | tf_op jit(solution)/shard_map/reduce_scatter | solution.py:43
  153.7 27.8 %reduce-scatter.5.cloned.1.call-done = f32[8,4,256]{2,0,1:T(8,128)} async-done(((f32[16,4,256]{2,0,1:T(8,128)}), f32[8,4,256]{2,0,1:T(8,128)}) %reduce-scatter.5.cloned.1.call-update) | async-done | bytes 32784 | tf_op jit(solution)/shard_map/reduce_scatter | solution.py:43
  182.3 20.7 %all-reduce.1 = f32[8,4,256]{2,1,0:T(4,128)S(1)} all-reduce(f32[8,4,256]{2,1,0:T(4,128)S(1)} %copy.30), channel_id=6, replica_groups=mesh['row_0'=8,'row_1'=4,'row_2'=2,'col'=16] {'row_0'}, use_global_device_ids=true, to_apply=%region_3.0.clone | all-reduce | flops 8192 | bytes 65536
  203.7 18.3 %all_gather.15 = f32[8,4,256]{2,1,0:T(4,128)S(1)} all-gather(f32[1,4,256]{2,1,0:T(4,128)S(1)} %constant_dynamic-slice_fusion.1), channel_id=1, replica_groups=mesh['row_0'=8,'row_1'=4,'row_2'=2,'col'=16] {'row_0'}, dimensions={0}, use_global_device_ids=true | all-gather | bytes 36864 | tf_op jit(solution)/shard_map/all_gather | solution.py:50
  222.0 14.7 %all-gather = f32[16,4,256]{2,0,1:T(8,128)S(1)} all-gather(f32[8,4,256]{2,0,1:T(8,128)S(1)} %copy.31), channel_id=2, replica_groups=mesh['row_0'=8,'row_1'=4,'row_2'=2,'col'=16] {'row_2'}, dimensions={0}, use_global_device_ids=true | all-gather | bytes 98304 | tf_op jit(solution)/shard_map/all_gather | solution.py:50
  236.6 10.2 %all-gather.1 = f32[8,8,4,256]{3,1,0,2:T(8,128)S(1)} all-gather(f32[2,8,4,256]{3,1,0,2:T(8,128)S(1)} %bitcast.57), channel_id=3, replica_groups=mesh['row_0'=8,'row_1'=4,'row_2'=2,'col'=16] {'row_1'}, dimensions={0}, use_global_device_ids=true | all-gather | bytes 327680 | tf_op jit(solution)/shard_map/all_gather | solution.py:50
  247.3 11.7 %cholesky.50 = f32[128,128]{1,0:T(8,128)S(1)} custom-call(f32[128,128]{1,0:T(8,128)S(1)} %cholesky.118), custom_call_target="Cholesky" | custom-call | tf_op jit(solution)/shard_map/jit(cholesky)/cholesky | solution.py:88
  259.1 9.8 %custom-call.14 = f32[1,128,128]{1,2,0:T(8,128)S(1)} custom-call(f32[1,128,128]{2,1,0:T(8,128)S(1)} %get-tuple-element.24), custom_call_target="InvertDiagBlocksLowerTriangular" | custom-call | tf_op jit(solution)/shard_map/jit(cholesky)/cholesky | solution.py:88
  269.4 11.7 %cholesky.105 = f32[128,128]{1,0:T(8,128)S(1)} custom-call(f32[128,128]{1,0:T(8,128)S(1)} %convolution_subtract_fusion.1), custom_call_target="Cholesky" | custom-call | tf_op jit(solution)/shard_map/jit(cholesky)/cholesky | solution.py:88
  283.2 4.1 while.1
  284.0 1.4 bitcast_dynamic-update-slice_fusion.2
  287.4 19.7 %custom-call.15 = f32[2,128,128]{1,2,0:T(8,128)S(1)} custom-call(f32[2,128,128]{2,1,0:T(8,128)S(1)} %get-tuple-element.10), custom_call_target="InvertDiagBlocksLowerTriangular" | custom-call | tf_op jit(solution)/shard_map/triangular_solve | solution.py:89
  308.0 1.5 fusion.14
  309.5 2.7 reshape.49
  312.2 49.0 %all_to_all.28 = f32[64,4,1536]{2,1,0:T(4,128)} all-to-all(f32[64,4,1536]{2,1,0:T(4,128)} %reshape.49), channel_id=1, replica_groups=mesh['row_0'=8,'row_1'=4,'row_2'=2,'col'=16] {'row_0','row_1','row_2'}, dimensions={0} | all-to-all | bytes 3145728 | tf_op jit(solution)/shard_map/all_to_all | solution.py:73
  361.2 1.7 reduce_sum.37
  363.0 23.9 %all_to_all.29 = f32[16,1,4]{2,1,0:T(1,128)S(1)} all-to-all(f32[16,1,4]{2,1,0:T(1,128)S(1)} %broadcast_in_dim.16), channel_id=1, replica_groups=mesh['row_0'=8,'row_1'=4,'row_2'=2,'col'=16] {'col'}, dimensions={0} | all-to-all | bytes 512 | tf_op jit(solution)/shard_map/all_to_all | solution.py:22
  387.6 7.8 %all-to-all-start.4 = ((f32[64,1,4]{2,1,0:T(1,128)}), f32[64,1,4]{2,1,0:T(1,128)S(1)}, u32[]{:S(2)}, u32[]{:S(2)}) async-start(f32[64,1,4]{2,1,0:T(1,128)} %broadcast_in_dim.18), calls=%async_computation.6 | async-start | bytes 65536 | tf_op jit(solution)/shard_map/all_to_all | solution.py:22
  395.4 9.3 %all-to-all-done.4 = f32[64,1,4]{2,1,0:T(1,128)S(1)} async-done(((f32[64,1,4]{2,1,0:T(1,128)}), f32[64,1,4]{2,1,0:T(1,128)S(1)}, u32[]{:S(2)}, u32[]{:S(2)}) %all-to-all-start.4) | async-done | bytes 1056 | tf_op jit(solution)/shard_map/all_to_all | solution.py:22
  405.8 4.8 %all-to-all-start.3 = ((bf16[64,4,1536]{2,1,0:T(4,128)(2,1)}), bf16[64,4,1536]{2,1,0:T(4,128)(2,1)S(1)}, u32[]{:S(2)}, u32[]{:S(2)}) async-start(bf16[64,4,1536]{2,1,0:T(4,128)(2,1)} %broadcast_in_dim.17), calls=%async_computation.5 | async-start | bytes 1572864 | tf_op jit(solution)/shard_map/all_to_all | solution.py:22
  411.9 21.8 %all-to-all-done.3 = bf16[64,4,1536]{2,1,0:T(4,128)(2,1)S(1)} async-done(((bf16[64,4,1536]{2,1,0:T(4,128)(2,1)}), bf16[64,4,1536]{2,1,0:T(4,128)(2,1)S(1)}, u32[]{:S(2)}, u32[]{:S(2)}) %all-to-all-start.3) | async-done | bytes 786464 | tf_op jit(solution)/shard_map/all_to_all | solution.py:22
  433.9 2.2 fusion.1
  (66 shorter events, 15.2 us)
Async XLA Ops:
  7.2 1.1 copy-start
  7.2 145.2 %reduce-scatter.3.cloned.1.call-start = ((), (), s32[]{:S(2)}) async-start(), calls=%async_computation.7 | async-start | bytes 327680 | tf_op jit(solution)/shard_map/reduce_scatter | solution.py:43
  121.1 60.4 %reduce-scatter.5.cloned.1.call-start = ((), (), s32[]{:S(2)}) async-start(), calls=%async_computation.8 | async-start | bytes 98304 | tf_op jit(solution)/shard_map/reduce_scatter | solution.py:43
  259.0 48.9 %copy-start.2 = (f32[128,1536]{1,0:T(8,128)S(1)}, f32[128,1536]{1,0:T(8,128)}, u32[]{:S(2)}) copy-start(f32[128,1536]{1,0:T(8,128)} %param.6) | copy-start | bytes 2359300
  259.1 48.9 %copy-start.3 = (bf16[128,1536]{1,0:T(8,128)(2,1)S(1)}, bf16[128,1536]{1,0:T(8,128)(2,1)}, u32[]{:S(2)}) copy-start(bf16[128,1536]{1,0:T(8,128)(2,1)} %param.5) | copy-start | bytes 1179652
  307.3 53.9 %copy-start.4 = (bf16[128,128]{0,1:T(8,128)(2,1)}, bf16[128,128]{0,1:T(8,128)(2,1)S(1)}, u32[]{:S(2)}) copy-start(bf16[128,128]{0,1:T(8,128)(2,1)S(1)} %get-tuple-element.27) | copy-start | bytes 98308
  307.9 4.3 copy-start.6
  387.6 17.1 %all-to-all-start.4 = ((f32[64,1,4]{2,1,0:T(1,128)}), f32[64,1,4]{2,1,0:T(1,128)S(1)}, u32[]{:S(2)}, u32[]{:S(2)}) async-start(f32[64,1,4]{2,1,0:T(1,128)} %broadcast_in_dim.18), calls=%async_computation.6 | async-start | bytes 65536 | tf_op jit(solution)/shard_map/all_to_all | solution.py:22
  405.8 27.9 %all-to-all-start.3 = ((bf16[64,4,1536]{2,1,0:T(4,128)(2,1)}), bf16[64,4,1536]{2,1,0:T(4,128)(2,1)S(1)}, u32[]{:S(2)}, u32[]{:S(2)}) async-start(bf16[64,4,1536]{2,1,0:T(4,128)(2,1)} %broadcast_in_dim.17), calls=%async_computation.5 | async-start | bytes 1572864 | tf_op jit(solution)/shard_map/all_to_all | solution.py:22
  433.9 3.3 copy-start.1
  433.9 2.3 copy-start.5
  433.9 2.3 copy-start.7
  433.9 2.3 copy-start.8
Sparse Core Ops, SparseCore 0:
  121.3 31.0 reduce-scatter.2
  155.7 25.8 reduce-scatter.4
where the time goes:
time: 445 us; the launch traced here: 444 us
  blocking collectives  246 us (55%)
  waiting for transfers between devices  90.2 us (20%)
  other arithmetic  56.5 us (13%)
  between operations  15.6 us (4%)
  local copies, waits for them, and re-layouts  14.5 us (3%)
  starting transfers between devices  12.6 us (3%)
  matrix products  8.13 us (2%)
    all_to_all x2, blocking collectives, sent_to_all(): return lax.all_to_all(copies, axis, split_axis=0, concat_axis=0, tiled=True)  134 us
    reduce_scatter x2, waiting for transfers between devices, own_block(): blocks = lax.psum_scatter(blocks, axes[k], scatter_dimension=0, tiled=True)  59 us
    all_to_all x1, blocking collectives, sum_at_owner(): lax.all_to_all(blocks, axis, split_axis=0, concat_axis=0, tiled=True)  49 us
    all_gather x3, blocking collectives, all_blocks(): blocks = lax.all_gather(blocks, axes[k])  43.2 us
    another operation x6, other arithmetic, orthonormalize(): chol_factor = jnp.linalg.cholesky(gram_matrix)  33.9 us
    all_to_all x2, waiting for transfers between devices, sent_to_all(): return lax.all_to_all(copies, axis, split_axis=0, concat_axis=0, tiled=True)  31.1 us
    unnamed x1, blocking collectives  20.7 us
    another operation x3, other arithmetic, orthonormalize(): lax.linalg.triangular_solve(chol_factor, left_rows, left_side=False, lowe...  19.7 us
  transfers between devices with their start and end apart: 4, of which 4 were waited for; matrix products, arithmetic and copies ran while one was open for 1% of the time, Pallas kernels for 0%

commit v1 on v0

v1 whole, which is shorter than its diff:
```python
import functools
import math

import jax
import jax.numpy as jnp
from jax import lax
from jax.experimental import pallas as pl
from jax.experimental.pallas import tpu as pltpu
from jax.sharding import PartitionSpec as P

epsilon = 1e-06
momentum_decay = 0.6
step_rate = 0.5

F32 = jnp.float32
BF16 = jnp.bfloat16
HI = lax.Precision.HIGHEST
MESH = pl.DeviceIdType.MESH
GROUP = 32


def tn(a, b):
    return lax.dot_general(a, b, (((0,), (0,)), ((), ())), precision=HI, preferred_element_type=F32)


def nt(a, b):
    return lax.dot_general(a, b, (((1,), (1,)), ((), ())), precision=HI, preferred_element_type=F32)


def spread(v, i):
    return jnp.broadcast_to(v[i : i + 1, :], (8, 128))


def fill(v, j):
    return jnp.broadcast_to(v[:, j : j + 1], (8, 128))


def small_inverse(p0):
    cols = [fill(p0, j) for j in range(8)]
    e = {(i, j): spread(cols[j], i) for j in range(8) for i in range(j, 8)}
    low, inv = {}, {}
    for j in range(8):
        r = lax.rsqrt(e[j, j])
        inv[j, j] = r
        for i in range(j + 1, 8):
            low[i, j] = e[i, j] * r
        for k in range(j + 1, 8):
            for i in range(k, 8):
                e[i, k] = e[i, k] - low[i, j] * low[k, j]
    for i in range(8):
        for j in range(i):
            s = low[i, j] * inv[j, j]
            for k in range(j + 1, i):
                s = s + low[i, k] * inv[k, j]
            inv[i, j] = -inv[i, i] * s
    return inv


def panel_step(t, panels, group):
    lane = lax.broadcasted_iota(jnp.int32, (8, 128), 1)
    sub = lax.broadcasted_iota(jnp.int32, (8, 128), 0)
    p = panels[0]
    p0, p1 = p[:, :128], p[:, 128:]
    inv = small_inverse(p0)
    a0 = jnp.where(lane < 8, (lane == sub).astype(F32), p0)
    q0, q1 = jnp.zeros((8, 128), F32), jnp.zeros((8, 128), F32)
    for j in range(8):
        col = jnp.zeros((8, 128), F32)
        for i in range(j, 8):
            col = jnp.where(sub == i, inv[i, j], col)
        q0 = q0 + col * spread(a0, j)
        q1 = q1 + col * spread(p1, j)
    r0 = [spread(q0, k) for k in range(8)]
    r1 = [spread(q1, k) for k in range(8)]
    out = []
    for s in range(1, group):
        b0, b1 = panels[s][:, :128], panels[s][:, 128:]
        live = t + s < group
        cols = [jnp.where(live, fill(b0, j), 0.0) for j in range(8)]
        b0 = jnp.where(jnp.logical_and(lane < 8, live), 0.0, b0)
        for k in range(8):
            m = cols[0] * inv[k, 0]
            for j in range(1, k + 1):
                m = m + cols[j] * inv[k, j]
            b0 = b0 - m * r0[k]
            b1 = b1 - m * r1[k]
        out.append(jnp.concatenate([b0, b1], axis=1))
    out.append(jnp.concatenate([q0, q1], axis=1))
    return tuple(pltpu.roll(v, 248, 1) for v in out)


def inverse_factor(work, size, rows, midway):
    group = rows // 8
    for ob in range(size // rows):
        lo = ob * rows
        if 2 * lo == size:
            midway()
        panels = tuple(work[lo + 8 * i : lo + 8 * i + 8, :] for i in range(group))
        panels = lax.fori_loop(0, group, lambda t, ps: panel_step(t, ps, group), panels)
        q = jnp.concatenate(panels, axis=0)
        rest = size - lo - rows
        lane = lax.broadcasted_iota(jnp.int32, (rows, size), 1)
        row = lax.broadcasted_iota(jnp.int32, (rows, size), 0)
        own = jnp.where(jnp.logical_or(lane < rest, lane > row + (size - rows)), 0.0, q)
        if ob:
            work[:lo, :] = pltpu.roll(work[:lo, :], size - rows, 1)
        work[lo : lo + rows, :] = own
        if rest:
            lane = lax.broadcasted_iota(jnp.int32, (rest, size), 1)
            old = jnp.where(lane < rows, 0.0, work[lo + rows :, :])
            both = jnp.where(lax.broadcasted_iota(jnp.int32, (rows, size), 1) < rest, q, own)
            work[lo + rows :, :] = pltpu.roll(old, size - rows, 1) - tn(q[:, :rest], both)


def far_first(k, n):
    h = (k + 1) // 2
    return n // 2 + h * (1 - 2 * (k % 2))


def take(ref, sem):
    pltpu.make_async_copy(ref, ref, sem).wait()


def exchange_kernel(
    sizes,
    gradient,
    momentum,
    basis,
    ortho_out,
    right_out,
    scale_out,
    grad_v,
    mom_v,
    basis_v,
    low,
    part,
    z_in,
    left,
    gram,
    gram_in,
    gram_own,
    gram_all,
    work,
    wide,
    core_in,
    core_sum,
    x_in,
    x_sum,
    y_in,
    right,
    square,
    square_z,
    square_own,
    square_r,
    load_sem,
    send_sem,
    recv_sem,
):
    ys, xs, zs, ff = sizes
    rows = ys * xs * 2
    half = ys * xs
    rank = 256
    r = lax.axis_index("row")
    c = lax.axis_index("col")
    core = lax.rem(r, 2)
    x = lax.rem(r // 2, xs)
    y = r // (2 * xs)
    owner = core * half + x * ys + y

    loads = [
        pltpu.make_async_copy(gradient, grad_v, load_sem.at[0]),
        pltpu.make_async_copy(momentum, mom_v, load_sem.at[1]),
        pltpu.make_async_copy(basis, basis_v, load_sem.at[2]),
    ]
    for copy in loads:
        copy.start()

    def send(src, dst, phase, row, col):
        pltpu.make_async_remote_copy(
            src_ref=src,
            dst_ref=dst,
            send_sem=send_sem.at[phase],
            recv_sem=recv_sem.at[phase],
            device_id=(row, col),
            device_id_type=MESH,
        ).start()

    def each_row(k, fn):
        d = far_first(k, rows)
        fn(d, lax.rem(r + d, rows))

    def each_col(k, fn):
        d = far_first(k, zs)
        fn(d, lax.rem(c + d, zs))

    def over_rows(fn):
        lax.fori_loop(0, rows - 1, lambda k, _: (each_row(k, fn), 0)[1], 0)

    def over_cols(fn):
        lax.fori_loop(0, zs - 1, lambda k, _: (each_col(k, fn), 0)[1], 0)

    barrier = pltpu.get_barrier_semaphore()
    over_cols(lambda d, p: pl.semaphore_signal(barrier, inc=1, device_id=(r, p), device_id_type=MESH))
    over_rows(lambda d, p: pl.semaphore_signal(barrier, inc=1, device_id=(p, c), device_id_type=MESH))

    for copy in loads:
        copy.wait()
    low[...] = (mom_v[...] + grad_v[...].astype(F32)).astype(BF16)
    local = lax.dot_general(
        low[...], basis_v[...], (((1,), (1,)), ((), ())), preferred_element_type=F32
    )
    part[...] = local.reshape(part.shape)
    pl.semaphore_wait(barrier, rows + zs - 2)

    over_cols(lambda d, p: send(part.at[p], z_in.at[d - 1], 0, r, p))
    mine = part[c]
    take(z_in, recv_sem.at[0])
    for k in range(zs - 1):
        mine = mine + z_in[k]
    left[c] = mine
    over_cols(lambda d, p: send(left.at[c], left.at[c], 1, r, p))
    take(z_in, recv_sem.at[1])

    left_rows = left[...].reshape(128, rank)
    whole = tn(left_rows, left_rows)
    each = 64 // rows
    for h in range(2):
        gram[h * 32 // each : (h + 1) * 32 // each] = whole[:, h * 128 : (h + 1) * 128].reshape(
            32 // each, each, 8, 128
        )
    over_rows(lambda d, p: send(gram.at[p], gram_in.at[d - 1], 2, p, c))

    high = left_rows.astype(BF16)
    rest = left_rows - high.astype(F32)
    middle = rest.astype(BF16)
    lowest = (rest - middle.astype(F32)).astype(BF16)
    count = rows // 4
    for q in range(4):
        cols = low[:, q * (ff // 4) : (q + 1) * (ff // 4)]
        block = sum(
            lax.dot_general(cols, t, (((0,), (0,)), ((), ())), preferred_element_type=F32)
            for t in (lowest, middle, high)
        )
        wide[q * count : (q + 1) * count] = block.reshape(count, ff // rows, rank)
    partner = r + 1 - 2 * core
    send(wide.at[pl.ds((1 - core) * half, half)], core_in, 3, partner, c)

    own = gram[r]
    take(gram_in, recv_sem.at[2])
    for k in range(rows - 1):
        own = own + gram_in[k]
    gram_own[...] = own
    gram_all[r] = own
    over_rows(lambda d, p: send(gram_own, gram_all.at[r], 4, p, c))

    take(core_in, recv_sem.at[3])
    core_sum[...] = core_in[...] + wide[pl.ds(core * half, half)]
    for d in range(1, xs):
        to = lax.rem(x + d, xs)
        send(core_sum.at[pl.ds(to * ys, ys)], x_in.at[d - 1], 5, (y * xs + to) * 2 + core, c)

    def middle_of_factor():
        take(x_in, recv_sem.at[5])
        total = core_sum[pl.ds(x * ys, ys)]
        for k in range(xs - 1):
            total = total + x_in[k]
        x_sum[...] = total

        def step(k, _):
            d = far_first(k, ys)
            to = lax.rem(y + d, ys)
            send(x_sum.at[to], y_in.at[d - 1], 6, (to * xs + x) * 2 + core, c)
            return 0

        lax.fori_loop(0, ys - 1, step, 0)

    take(gram_in, recv_sem.at[4])
    for h in range(2):
        work[:, h * 128 : (h + 1) * 128] = gram_all[h * 32 // each : (h + 1) * 32 // each].reshape(rank, 128)
    inverse_factor(work, rank, GROUP, middle_of_factor)

    take(y_in, recv_sem.at[6])
    slice_sum = x_sum[y]
    for k in range(ys - 1):
        slice_sum = slice_sum + y_in[k]
    inverse = work[...]
    mine = nt(slice_sum, inverse)
    right[owner] = mine.astype(BF16)
    square[...] = jnp.sum(mine * mine, axis=0, keepdims=True)
    over_cols(lambda d, p: send(square, square_z.at[d - 1], 7, r, p))

    def step(k, _):
        to = lax.rem(y + far_first(k, ys), ys)
        send(right.at[owner], right.at[owner], 8, (to * xs + x) * 2 + core, c)
        return 0

    lax.fori_loop(0, ys - 1, step, 0)

    ortho_out[...] = nt(left_rows, inverse).astype(BF16)

    take(square_z, recv_sem.at[7])
    total = square[...]
    for k in range(zs - 1):
        total = total + square_z[k]
    square_own[...] = total
    over_rows(lambda d, p: send(square_own, square_r.at[d - 1], 9, p, c))

    take(right.at[pl.ds(0, ys - 1)], recv_sem.at[8])
    block = pl.ds(core * half + x * ys, ys)
    for d in range(1, xs):
        to = lax.rem(x + d, xs)
        send(right.at[block], right.at[block], 10, (y * xs + to) * 2 + core, c)
    take(right.at[pl.ds(0, (xs - 1) * ys)], recv_sem.at[10])
    block = pl.ds(core * half, half)
    send(right.at[block], right.at[block], 11, partner, c)

    take(square_r, recv_sem.at[9])
    for k in range(rows - 1):
        total = total + square_r[k]
    scale_out[...] = jnp.sqrt(total / (ff * zs) + epsilon)
    take(right.at[pl.ds(0, half)], recv_sem.at[11])
    right_out[...] = right[...]

    take(z_in, send_sem.at[0])
    take(z_in, send_sem.at[1])
    take(gram_in, send_sem.at[2])
    take(core_in, send_sem.at[3])
    take(gram_in, send_sem.at[4])
    take(x_in, send_sem.at[5])
    take(y_in, send_sem.at[6])
    take(square_z, send_sem.at[7])
    take(right.at[pl.ds(0, ys - 1)], send_sem.at[8])
    take(square_r, send_sem.at[9])
    take(right.at[pl.ds(0, (xs - 1) * ys)], send_sem.at[10])
    take(right.at[pl.ds(0, half)], send_sem.at[11])


def finish_kernel(factor, weight, gradient, momentum, ortho, right, scale, weight_out, momentum_out, basis_out):
    cols = weight.shape[1]
    col_scale = scale[...]
    basis = right[...].astype(F32).reshape(cols, 256) / col_scale
    basis_low = basis.astype(BF16)
    basis_out[...] = basis_low.astype(F32).T.astype(BF16)
    rows = ortho[...]
    scaled = (rows.astype(F32) * col_scale).astype(BF16)
    dims = (((1,), (1,)), ((), ()))
    correction = lax.dot_general(scaled, basis_low, dims, preferred_element_type=F32)
    change = lax.dot_general(rows, basis_low, dims, preferred_element_type=F32)
    buffer = momentum[...] + gradient[...].astype(F32)
    momentum_out[...] = buffer - (1.0 - momentum_decay) * correction
    weight_out[...] = (weight[...].astype(F32) - factor * change).astype(BF16)


def per_device(sizes, dims, weight, gradient, momentum, old_basis):
    ys, xs, zs, ff = sizes
    rows, half, cut, lines = ys * xs * 2, ys * xs, ff // (ys * xs * 2), 128 // zs
    each = 64 // rows
    anywhere = pl.BlockSpec(memory_space=pl.ANY)
    inside = pl.BlockSpec(memory_space=pltpu.VMEM)
    ortho, right, scale = pl.pallas_call(
        functools.partial(exchange_kernel, sizes),
        out_shape=(
            jax.ShapeDtypeStruct((128, 256), BF16),
            jax.ShapeDtypeStruct((rows, cut, 256), BF16),
            jax.ShapeDtypeStruct((1, 256), F32),
        ),
        in_specs=[anywhere] * 3,
        out_specs=(inside, inside, inside),
        scratch_shapes=[
            pltpu.VMEM((128, ff), BF16),
            pltpu.VMEM((128, ff), F32),
            pltpu.VMEM((256, ff), BF16),
            pltpu.VMEM((128, ff), BF16),
            pltpu.VMEM((zs, lines, 256), F32),
            pltpu.VMEM((zs - 1, lines, 256), F32),
            pltpu.VMEM((zs, lines, 256), F32),
            pltpu.VMEM((rows, each, 8, 128), F32),
            pltpu.VMEM((rows - 1, each, 8, 128), F32),
            pltpu.VMEM((each, 8, 128), F32),
            pltpu.VMEM((rows, each, 8, 128), F32),
            pltpu.VMEM((256, 256), F32),
            pltpu.VMEM((rows, cut, 256), F32),
            pltpu.VMEM((half, cut, 256), F32),
            pltpu.VMEM((half, cut, 256), F32),
            pltpu.VMEM((xs - 1, ys, cut, 256), F32),
            pltpu.VMEM((ys, cut, 256), F32),
            pltpu.VMEM((ys - 1, cut, 256), F32),
            pltpu.VMEM((rows, cut, 256), BF16),
            pltpu.VMEM((1, 256), F32),
            pltpu.VMEM((zs - 1, 1, 256), F32),
            pltpu.VMEM((1, 256), F32),
            pltpu.VMEM((rows - 1, 1, 256), F32),
            pltpu.SemaphoreType.DMA((3,)),
            pltpu.SemaphoreType.DMA((12,)),
            pltpu.SemaphoreType.DMA((12,)),
        ],
        compiler_params=pltpu.CompilerParams(
            collective_id=0, has_side_effects=True, vmem_limit_bytes=40 * 1024 * 1024
        ),
    )(gradient, momentum, old_basis)
    total_rows, _ = dims
    factor = step_rate * math.sqrt(total_rows / 256)
    steps = 4
    wide = ff // steps
    strip = lambda n: pl.BlockSpec((n, wide), lambda i: (0, i))
    return pl.pallas_call(
        functools.partial(finish_kernel, factor),
        grid=(steps,),
        out_shape=(
            jax.ShapeDtypeStruct((128, ff), BF16),
            jax.ShapeDtypeStruct((128, ff), F32),
            jax.ShapeDtypeStruct((256, ff), BF16),
        ),
        in_specs=[
            strip(128),
            strip(128),
            strip(128),
            pl.BlockSpec((128, 256), lambda i: (0, 0)),
            pl.BlockSpec((rows // steps, cut, 256), lambda i: (i, 0, 0)),
            pl.BlockSpec((1, 256), lambda i: (0, 0)),
        ],
        out_specs=(strip(128), strip(128), strip(256)),
    )(weight, gradient, momentum, ortho, right, scale)


def solution(mesh, xs=4):
    rows, zs = mesh.shape["row"], mesh.shape["col"]
    sizes = (rows // (2 * xs), xs, zs, 1536)
    return jax.shard_map(
        functools.partial(per_device, sizes, (128 * rows, 1536 * zs)),
        mesh=mesh,
        in_specs=(P("row", "col"), P("row", "col"), P("row", "col"), P(None, "col")),
        out_specs=(P("row", "col"), P("row", "col"), P(None, "col")),
        check_vma=False,
    )
```

time: 445 us -> 101 us (0.23)
  blocking collectives: 246 us -> 0 us
  Pallas kernels: 0 us -> 95 us
  waiting for transfers between devices: 90.2 us -> 0 us
  other arithmetic: 56.5 us -> 0 us
  between operations: 15.6 us -> 0.66 us
  starting transfers between devices: 12.6 us -> 0 us
  local copies, waits for them, and re-layouts: 14.5 us -> 5.3 us
  matrix products: 8.13 us -> 0 us
    all_to_all x3 -> x0, blocking collectives: 182 us -> none  [the longest x2 134 us: sent_to_all(): return lax.all_to_all(copies, axis, split_axis=0, concat_axis=0, tiled=True)]
    pallas_call x0 -> x2, Pallas kernels: none -> 95 us  [the longest x1 90.7 us: per_device(): pl.pallas_call(functools.partial(exchange_kernel, sizes), out_shape=(jax....]
    reduce_scatter x2 -> x0, waiting for transfers between devices: 59 us -> none  [own_block(): blocks = lax.psum_scatter(blocks, axes[k], scatter_dimension=0, tiled=True)]
    another operation x9 -> x0, other arithmetic: 53.7 us -> none  [the longest x6 33.9 us: orthonormalize(): chol_factor = jnp.linalg.cholesky(gram_matrix)]
    all_gather x3 -> x0, blocking collectives: 43.2 us -> none  [all_blocks(): blocks = lax.all_gather(blocks, axes[k])]
    all_to_all x2 -> x0, waiting for transfers between devices: 31.1 us -> none  [sent_to_all(): return lax.all_to_all(copies, axis, split_axis=0, concat_axis=0, tiled=True)]
    unnamed x1 -> x0, blocking collectives: 20.7 us -> none
    all_to_all x2 -> x0, starting transfers between devices: 12.5 us -> none  [sent_to_all(): return lax.all_to_all(copies, axis, split_axis=0, concat_axis=0, tiled=True)]
  transfers between devices with their start and end apart: 4 -> 0, of which waited for: 4 -> 0; matrix products, arithmetic and copies ran while one was open for 1% -> 0% of each run, Pallas kernels for 0% -> 0%
where the time goes in v1:
time: 101 us
  Pallas kernels  95 us (94%)
  local copies, waits for them, and re-layouts  5.3 us (5%)
    pallas_call x1, Pallas kernels, per_device(): pl.pallas_call(functools.partial(exchange_kernel, sizes), out_shape=(jax....  90.7 us
    unnamed x12, local copies, waits for them, and re-layouts  5.3 us
    pallas_call x1, Pallas kernels, per_device(): pl.pallas_call(functools.partial(finish_kernel, factor), grid=(steps,), o...  4.28 us

profile of v1, /device:TPU:1, one launch (start us, length us, event | category | flops | bytes accessed | tf_op | source)
XLA Modules:
  0.0 101.0 jit_solution(14900431081227004698)
XLA Ops:
  0.6 0.0 copy-start
  0.6 1.1 %copy-done = f32[128,1536]{1,0:T(8,128)S(1)} copy-done((f32[128,1536]{1,0:T(8,128)S(1)}, f32[128,1536]{1,0:T(8,128)}, u32[]{:S(2)}) %copy-start) | copy-done | bytes 786456
  1.8 0.0 copy-start.1
  1.8 1.0 copy-done.1
  2.8 0.0 copy-start.2
  2.8 1.1 %copy-done.2 = bf16[256,1536]{1,0:T(8,128)(2,1)S(1)} copy-done((bf16[256,1536]{1,0:T(8,128)(2,1)S(1)}, bf16[256,1536]{1,0:T(8,128)(2,1)}, u32[]{:S(2)}) %copy-start.2) | copy-done | bytes 786456
  3.9 90.7 %shard_map.67 = (bf16[128,256]{1,0:T(8,128)(2,1)S(1)}, bf16[64,24,256]{2,1,0:T(8,128)(2,1)S(1)}, f32[1,256]{1,0:T(1,128)S(1)}) custom-call(bf16[128,1536]{1,0:T(8,128)(2,1)S(1)} %copy-done.1, f32[128,1536]{1,0:T(8,128)S(1)} %copy-done, bf16[256,1536]{1,0:T(8,128)(2,1)S(1)} %copy-done.2), custom_call_target="tpu_custom_call" | custom-call | tf_op jit(solution)/shard_map/pallas_call | solution.py:360
  94.6 0.0 copy-start.3
  94.6 0.9 copy-done.3
  95.5 0.0 copy-start.4
  95.5 0.6 copy-done.4
  96.1 0.0 copy-start.5
  96.1 0.5 copy-done.5
  96.7 4.3 %shard_map.68 = (bf16[128,1536]{1,0:T(8,128)(2,1)}, f32[128,1536]{1,0:T(8,128)}, bf16[256,1536]{1,0:T(8,128)(2,1)}) custom-call(bf16[128,1536]{1,0:T(8,128)(2,1)} %weight.1, bf16[128,1536]{1,0:T(8,128)(2,1)} %gradient.3, f32[128,1536]{1,0:T(8,128)} %momentum.3, bf16[128,256]{1,0:T(8,128)(2,1)} %copy-done.4, bf16[64,24,256]{2,1,0:T(8,128)(2,1)} %copy-done.3, ...), custom_call_target="tpu_custom_call" | custom-call | tf_op jit(solution)/shard_map/pallas_call | solution.py:406
Async XLA Ops:
  0.6 1.1 %copy-start = (f32[128,1536]{1,0:T(8,128)S(1)}, f32[128,1536]{1,0:T(8,128)}, u32[]{:S(2)}) copy-start(f32[128,1536]{1,0:T(8,128)} %momentum.3) | copy-start | bytes 2359300
  1.8 1.0 copy-start.1
  2.8 1.1 %copy-start.2 = (bf16[256,1536]{1,0:T(8,128)(2,1)S(1)}, bf16[256,1536]{1,0:T(8,128)(2,1)}, u32[]{:S(2)}) copy-start(bf16[256,1536]{1,0:T(8,128)(2,1)} %basis.1) | copy-start | bytes 2359300
  94.6 0.9 copy-start.3
  95.5 0.6 copy-start.4
  96.1 0.5 copy-start.5

commit v2 on v1

--- a/solution.py
+++ b/solution.py
@@ -17,22 +17,42 @@
 HI = lax.Precision.HIGHEST
 MESH = pl.DeviceIdType.MESH
 GROUP = 32
-
-
-def tn(a, b):
-    return lax.dot_general(a, b, (((0,), (0,)), ((), ())), precision=HI, preferred_element_type=F32)
+VMEM = 67043328
 
 
 def nt(a, b):
     return lax.dot_general(a, b, (((1,), (1,)), ((), ())), precision=HI, preferred_element_type=F32)
 
 
+def parts(a):
+    high = a.astype(BF16)
+    rest = a - high.astype(F32)
+    middle = rest.astype(BF16)
+    return high, middle, (rest - middle.astype(F32)).astype(BF16)
+
+
+def tn6(a, b):
+    ah, am, al = parts(a)
+    bh, bm, bl = parts(b)
+    left = jnp.concatenate([al, am, ah, am, ah, ah], axis=0)
+    right = jnp.concatenate([bh, bm, bl, bh, bm, bh], axis=0)
+    return lax.dot_general(left, right, (((0,), (0,)), ((), ())), preferred_element_type=F32)
+
+
 def spread(v, i):
     return jnp.broadcast_to(v[i : i + 1, :], (8, 128))
 
 
 def fill(v, j):
     return jnp.broadcast_to(v[:, j : j + 1], (8, 128))
+
+
+def tree(terms):
+    terms = list(terms)
+    while len(terms) > 1:
+        pairs = [a + b for a, b in zip(terms[::2], terms[1::2])]
+        terms = pairs + terms[len(pairs) * 2 :]
+    return terms[0]
 
 
 def small_inverse(p0):
@@ -49,10 +69,7 @@
                 e[i, k] = e[i, k] - low[i, j] * low[k, j]
     for i in range(8):
         for j in range(i):
-            s = low[i, j] * inv[j, j]
-            for k in range(j + 1, i):
-                s = s + low[i, k] * inv[k, j]
-            inv[i, j] = -inv[i, i] * s
+            inv[i, j] = -inv[i, i] * tree(low[i, k] * inv[k, j] for k in range(j, i))
     return inv
 
 
@@ -63,13 +80,14 @@
     p0, p1 = p[:, :128], p[:, 128:]
     inv = small_inverse(p0)
     a0 = jnp.where(lane < 8, (lane == sub).astype(F32), p0)
-    q0, q1 = jnp.zeros((8, 128), F32), jnp.zeros((8, 128), F32)
+    columns = []
     for j in range(8):
         col = jnp.zeros((8, 128), F32)
         for i in range(j, 8):
             col = jnp.where(sub == i, inv[i, j], col)
-        q0 = q0 + col * spread(a0, j)
-        q1 = q1 + col * spread(p1, j)
+        columns.append(col)
+    q0 = tree(columns[j] * spread(a0, j) for j in range(8))
+    q1 = tree(columns[j] * spread(p1, j) for j in range(8))
     r0 = [spread(q0, k) for k in range(8)]
     r1 = [spread(q1, k) for k in range(8)]
     out = []
@@ -78,12 +96,9 @@
         live = t + s < group
         cols = [jnp.where(live, fill(b0, j), 0.0) for j in range(8)]
         b0 = jnp.where(jnp.logical_and(lane < 8, live), 0.0, b0)
-        for k in range(8):
-            m = cols[0] * inv[k, 0]
-            for j in range(1, k + 1):
-                m = m + cols[j] * inv[k, j]
-            b0 = b0 - m * r0[k]
-            b1 = b1 - m * r1[k]
+        ms = [tree(cols[j] * inv[k, j] for j in range(k + 1)) for k in range(8)]
+        b0 = b0 - tree(ms[k] * r0[k] for k in range(8))
+        b1 = b1 - tree(ms[k] * r1[k] for k in range(8))
         out.append(jnp.concatenate([b0, b1], axis=1))
     out.append(jnp.concatenate([q0, q1], axis=1))
     return tuple(pltpu.roll(v, 248, 1) for v in out)
@@ -109,9 +124,7 @@
             lane = lax.broadcasted_iota(jnp.int32, (rest, size), 1)
             old = jnp.where(lane < rows, 0.0, work[lo + rows :, :])
             both = jnp.where(lax.broadcasted_iota(jnp.int32, (rows, size), 1) < rest, q, own)
-            work[lo + rows :, :] = pltpu.roll(old, size - rows, 1) - tn(q[:, :rest], both)
-
-
+            work[lo + rows :, :] = pltpu.roll(old, size - rows, 1) - tn6(q[:, :rest], both)
 def far_first(k, n):
     h = (k + 1) // 2
     return n // 2 + h * (1 - 2 * (k % 2))
@@ -152,6 +165,10 @@
     square_z,
     square_own,
     square_r,
+    square_half,
+    square_core,
+    gram_core,
+    gram_pair,
     load_sem,
     send_sem,
     recv_sem,
@@ -166,6 +183,8 @@
     x = lax.rem(r // 2, xs)
     y = r // (2 * xs)
     owner = core * half + x * ys + y
+    chip = r // 2
+    partner = r + 1 - 2 * core
 
     loads = [
         pltpu.make_async_copy(gradient, grad_v, load_sem.at[0]),
@@ -174,6 +193,16 @@
     ]
     for copy in loads:
         copy.start()
+
+    def drain(upto):
+        sent = [
+            z_in, z_in, gram_core, core_in, gram_in, x_in, y_in, square_z,
+            right.at[pl.ds(0, ys - 1)], square_r.at[pl.ds(0, half - 1)],
+            right.at[pl.ds(0, (xs - 1) * ys)], right.at[pl.ds(0, half)],
+            gram_in, gram_core, square_core,
+        ]
+        for phase in range(upto):
+            take(sent[phase], send_sem.at[phase])
 
     def send(src, dst, phase, row, col):
         pltpu.make_async_remote_copy(
@@ -185,23 +214,24 @@
             device_id_type=MESH,
         ).start()
 
-    def each_row(k, fn):
-        d = far_first(k, rows)
-        fn(d, lax.rem(r + d, rows))
+    def each_chip(k, fn):
+        d = far_first(k, half)
+        fn(d, 2 * lax.rem(chip + d, half) + core)
 
     def each_col(k, fn):
         d = far_first(k, zs)
         fn(d, lax.rem(c + d, zs))
 
-    def over_rows(fn):
-        lax.fori_loop(0, rows - 1, lambda k, _: (each_row(k, fn), 0)[1], 0)
+    def over_chips(fn):
+        lax.fori_loop(0, half - 1, lambda k, _: (each_chip(k, fn), 0)[1], 0)
 
     def over_cols(fn):
         lax.fori_loop(0, zs - 1, lambda k, _: (each_col(k, fn), 0)[1], 0)
 
     barrier = pltpu.get_barrier_semaphore()
     over_cols(lambda d, p: pl.semaphore_signal(barrier, inc=1, device_id=(r, p), device_id_type=MESH))
-    over_rows(lambda d, p: pl.semaphore_signal(barrier, inc=1, device_id=(p, c), device_id_type=MESH))
+    over_chips(lambda d, p: pl.semaphore_signal(barrier, inc=1, device_id=(p, c), device_id_type=MESH))
+    pl.semaphore_signal(barrier, inc=1, device_id=(partner, c), device_id_type=MESH)
 
     for copy in loads:
         copy.wait()
@@ -210,7 +240,7 @@
         low[...], basis_v[...], (((1,), (1,)), ((), ())), preferred_element_type=F32
     )
     part[...] = local.reshape(part.shape)
-    pl.semaphore_wait(barrier, rows + zs - 2)
+    pl.semaphore_wait(barrier, half + zs - 1)
 
     over_cols(lambda d, p: send(part.at[p], z_in.at[d - 1], 0, r, p))
     mine = part[c]
@@ -222,13 +252,15 @@
     take(z_in, recv_sem.at[1])
 
     left_rows = left[...].reshape(128, rank)
-    whole = tn(left_rows, left_rows)
-    each = 64 // rows
+    whole = tn6(left_rows, left_rows)
+    each = 32 // half
     for h in range(2):
-        gram[h * 32 // each : (h + 1) * 32 // each] = whole[:, h * 128 : (h + 1) * 128].reshape(
-            32 // each, each, 8, 128
-        )
-    over_rows(lambda d, p: send(gram.at[p], gram_in.at[d - 1], 2, p, c))
+        gram[h * half : (h + 1) * half] = whole[:, h * 128 : (h + 1) * 128].reshape(half, each, 8, 128)
+    send(gram.at[pl.ds((1 - core) * half, half)], gram_core, 2, partner, c)
+
+    take(gram_core, recv_sem.at[2])
+    gram_pair[...] = gram_core[...] + gram[pl.ds(core * half, half)]
+    over_chips(lambda d, p: send(gram_pair.at[p // 2], gram_in.at[d - 1], 12, p, c))
 
     high = left_rows.astype(BF16)
     rest = left_rows - high.astype(F32)
@@ -242,16 +274,16 @@
             for t in (lowest, middle, high)
         )
         wide[q * count : (q + 1) * count] = block.reshape(count, ff // rows, rank)
-    partner = r + 1 - 2 * core
     send(wide.at[pl.ds((1 - core) * half, half)], core_in, 3, partner, c)
 
-    own = gram[r]
-    take(gram_in, recv_sem.at[2])
-    for k in range(rows - 1):
+    take(gram_in, recv_sem.at[12])
+    own = gram_pair[chip]
+    for k in range(half - 1):
         own = own + gram_in[k]
     gram_own[...] = own
-    gram_all[r] = own
-    over_rows(lambda d, p: send(gram_own, gram_all.at[r], 4, p, c))
+    mine = core * half + chip
+    gram_all[mine] = own
+    over_chips(lambda d, p: send(gram_own, gram_all.at[mine], 4, p, c))
 
     take(core_in, recv_sem.at[3])
     core_sum[...] = core_in[...] + wide[pl.ds(core * half, half)]
@@ -275,8 +307,11 @@
         lax.fori_loop(0, ys - 1, step, 0)
 
     take(gram_in, recv_sem.at[4])
+    block = pl.ds(core * half, half)
+    send(gram_all.at[block], gram_all.at[block], 13, partner, c)
+    take(gram_core, recv_sem.at[13])
     for h in range(2):
-        work[:, h * 128 : (h + 1) * 128] = gram_all[h * 32 // each : (h + 1) * 32 // each].reshape(rank, 128)
+        work[:, h * 128 : (h + 1) * 128] = gram_all[h * half : (h + 1) * half].reshape(rank, 128)
     inverse_factor(work, rank, GROUP, middle_of_factor)
 
     take(y_in, recv_sem.at[6])
@@ -303,7 +338,8 @@
     for k in range(zs - 1):
         total = total + square_z[k]
     square_own[...] = total
-    over_rows(lambda d, p: send(square_own, square_r.at[d - 1], 9, p, c))
+    square_r[chip] = total
+    over_chips(lambda d, p: send(square_own, square_r.at[chip], 9, p, c))
 
     take(right.at[pl.ds(0, ys - 1)], recv_sem.at[8])
     block = pl.ds(core * half + x * ys, ys)
@@ -314,25 +350,19 @@
     block = pl.ds(core * half, half)
     send(right.at[block], right.at[block], 11, partner, c)
 
-    take(square_r, recv_sem.at[9])
-    for k in range(rows - 1):
+    take(square_r.at[pl.ds(0, half - 1)], recv_sem.at[9])
+    total = square_r[0]
+    for k in range(1, half):
         total = total + square_r[k]
+    square_half[...] = total
+    send(square_half, square_core, 14, partner, c)
+    take(square_core, recv_sem.at[14])
+    total = total + square_core[...]
     scale_out[...] = jnp.sqrt(total / (ff * zs) + epsilon)
     take(right.at[pl.ds(0, half)], recv_sem.at[11])
     right_out[...] = right[...]
 
-    take(z_in, send_sem.at[0])
-    take(z_in, send_sem.at[1])
-    take(gram_in, send_sem.at[2])
-    take(core_in, send_sem.at[3])
-    take(gram_in, send_sem.at[4])
-    take(x_in, send_sem.at[5])
-    take(y_in, send_sem.at[6])
-    take(square_z, send_sem.at[7])
-    take(right.at[pl.ds(0, ys - 1)], send_sem.at[8])
-    take(square_r, send_sem.at[9])
-    take(right.at[pl.ds(0, (xs - 1) * ys)], send_sem.at[10])
-    take(right.at[pl.ds(0, half)], send_sem.at[11])
+    drain(15)
 
 
 def finish_kernel(factor, weight, gradient, momentum, ortho, right, scale, weight_out, momentum_out, basis_out):
@@ -340,7 +370,7 @@
     col_scale = scale[...]
     basis = right[...].astype(F32).reshape(cols, 256) / col_scale
     basis_low = basis.astype(BF16)
-    basis_out[...] = basis_low.astype(F32).T.astype(BF16)
+    basis_out[...] = basis_low.T
     rows = ortho[...]
     scaled = (rows.astype(F32) * col_scale).astype(BF16)
     dims = (((1,), (1,)), ((), ()))
@@ -354,7 +384,7 @@
 def per_device(sizes, dims, weight, gradient, momentum, old_basis):
     ys, xs, zs, ff = sizes
     rows, half, cut, lines = ys * xs * 2, ys * xs, ff // (ys * xs * 2), 128 // zs
-    each = 64 // rows
+    each = 32 // half
     anywhere = pl.BlockSpec(memory_space=pl.ANY)
     inside = pl.BlockSpec(memory_space=pltpu.VMEM)
     ortho, right, scale = pl.pallas_call(
@@ -375,7 +405,7 @@
             pltpu.VMEM((zs - 1, lines, 256), F32),
             pltpu.VMEM((zs, lines, 256), F32),
             pltpu.VMEM((rows, each, 8, 128), F32),
-            pltpu.VMEM((rows - 1, each, 8, 128), F32),
+            pltpu.VMEM((half - 1, each, 8, 128), F32),
             pltpu.VMEM((each, 8, 128), F32),
             pltpu.VMEM((rows, each, 8, 128), F32),
             pltpu.VMEM((256, 256), F32),
@@ -389,18 +419,22 @@
             pltpu.VMEM((1, 256), F32),
             pltpu.VMEM((zs - 1, 1, 256), F32),
             pltpu.VMEM((1, 256), F32),
-            pltpu.VMEM((rows - 1, 1, 256), F32),
+            pltpu.VMEM((half, 1, 256), F32),
+            pltpu.VMEM((1, 256), F32),
+            pltpu.VMEM((1, 256), F32),
+            pltpu.VMEM((half, each, 8, 128), F32),
+            pltpu.VMEM((half, each, 8, 128), F32),
             pltpu.SemaphoreType.DMA((3,)),
-            pltpu.SemaphoreType.DMA((12,)),
-            pltpu.SemaphoreType.DMA((12,)),
+            pltpu.SemaphoreType.DMA((15,)),
+            pltpu.SemaphoreType.DMA((15,)),
         ],
         compiler_params=pltpu.CompilerParams(
-            collective_id=0, has_side_effects=True, vmem_limit_bytes=40 * 1024 * 1024
+            collective_id=0, has_side_effects=True, vmem_limit_bytes=VMEM
         ),
     )(gradient, momentum, old_basis)
     total_rows, _ = dims
     factor = step_rate * math.sqrt(total_rows / 256)
-    steps = 4
+    steps = 2
     wide = ff // steps
     strip = lambda n: pl.BlockSpec((n, wide), lambda i: (0, i))
     return pl.pallas_call(
@@ -420,6 +454,7 @@
             pl.BlockSpec((1, 256), lambda i: (0, 0)),
         ],
         out_specs=(strip(128), strip(128), strip(256)),
+        compiler_params=pltpu.CompilerParams(vmem_limit_bytes=VMEM),
     )(weight, gradient, momentum, ortho, right, scale)
 
 

time: 101 us -> 91.9 us (0.910)
  local copies, waits for them, and re-layouts: 5.3 us -> 0 us
  Pallas kernels: 95 us -> 91.1 us
    unnamed x12 -> x0, local copies, waits for them, and re-layouts: 5.3 us -> none
    pallas_call x1, Pallas kernels: 90.7 us -> 87.9 us  [per_device(): pl.pallas_call(functools.partial(exchange_kernel, sizes), out_shape=(jax....]
    pallas_call x1, Pallas kernels: 4.28 us -> 3.15 us  [per_device(): pl.pallas_call(functools.partial(finish_kernel, factor), grid=(steps,), o...]
where the time goes in v2:
time: 91.9 us; the launch traced here: 91.7 us
  Pallas kernels  91.1 us (99%)
    pallas_call x1, Pallas kernels, per_device(): pl.pallas_call(functools.partial(exchange_kernel, sizes), out_shape=(jax....  87.9 us
    pallas_call x1, Pallas kernels, per_device(): pl.pallas_call(functools.partial(finish_kernel, factor), grid=(steps,), o...  3.15 us

profile of v2, /device:TPU:1, one launch (start us, length us, event | category | flops | bytes accessed | tf_op | source)
XLA Modules:
  0.0 91.7 jit_solution(3803633414446225331)
XLA Ops:
  0.6 87.9 %shard_map.67 = (bf16[128,256]{1,0:T(8,128)(2,1)}, bf16[64,24,256]{2,1,0:T(8,128)(2,1)}, f32[1,256]{1,0:T(1,128)}) custom-call(bf16[128,1536]{1,0:T(8,128)(2,1)} %gradient.3, f32[128,1536]{1,0:T(8,128)} %momentum.3, bf16[256,1536]{1,0:T(8,128)(2,1)} %basis.1), custom_call_target="tpu_custom_call" | custom-call | tf_op jit(solution)/shard_map/pallas_call | solution.py:390
  88.6 3.1 %shard_map.68 = (bf16[128,1536]{1,0:T(8,128)(2,1)}, f32[128,1536]{1,0:T(8,128)}, bf16[256,1536]{1,0:T(8,128)(2,1)}) custom-call(bf16[128,1536]{1,0:T(8,128)(2,1)} %weight.1, bf16[128,1536]{1,0:T(8,128)(2,1)} %gradient.3, f32[128,1536]{1,0:T(8,128)} %momentum.3, bf16[128,256]{1,0:T(8,128)(2,1)} %get-tuple-element.6.ortho, ...), custom_call_target="tpu_custom_call" | custom-call | tf_op jit(solution)/shard_map/pallas_call | solution.py:440

commit v3 on v2

--- a/solution.py
+++ b/solution.py
@@ -333,6 +333,12 @@
 
     ortho_out[...] = nt(left_rows, inverse).astype(BF16)
 
+    take(right.at[pl.ds(0, ys - 1)], recv_sem.at[8])
+    block = pl.ds(core * half + x * ys, ys)
+    for d in range(1, xs):
+        to = lax.rem(x + d, xs)
+        send(right.at[block], right.at[block], 10, (y * xs + to) * 2 + core, c)
+
     take(square_z, recv_sem.at[7])
     total = square[...]
     for k in range(zs - 1):
@@ -341,11 +347,6 @@
     square_r[chip] = total
     over_chips(lambda d, p: send(square_own, square_r.at[chip], 9, p, c))
 
-    take(right.at[pl.ds(0, ys - 1)], recv_sem.at[8])
-    block = pl.ds(core * half + x * ys, ys)
-    for d in range(1, xs):
-        to = lax.rem(x + d, xs)
-        send(right.at[block], right.at[block], 10, (y * xs + to) * 2 + core, c)
     take(right.at[pl.ds(0, (xs - 1) * ys)], recv_sem.at[10])
     block = pl.ds(core * half, half)
     send(right.at[block], right.at[block], 11, partner, c)

time: 91.9 us -> 89.9 us (0.978)
  Pallas kernels: 91.1 us -> 89 us
    pallas_call x1, Pallas kernels: 87.9 us -> 85.9 us  [per_device(): pl.pallas_call(functools.partial(exchange_kernel, sizes), out_shape=(jax....]
where the time goes in v3:
time: 89.9 us; the launch traced here: 89.7 us
  Pallas kernels  89 us (99%)
    pallas_call x1, Pallas kernels, per_device(): pl.pallas_call(functools.partial(exchange_kernel, sizes), out_shape=(jax....  85.9 us
    pallas_call x1, Pallas kernels, per_device(): pl.pallas_call(functools.partial(finish_kernel, factor), grid=(steps,), o...  3.15 us

profile of v3, /device:TPU:1, one launch (start us, length us, event | category | flops | bytes accessed | tf_op | source)
XLA Modules:
  0.0 89.7 jit_solution(15160516682540624799)
XLA Ops:
  0.6 85.9 %shard_map.67 = (bf16[128,256]{1,0:T(8,128)(2,1)}, bf16[64,24,256]{2,1,0:T(8,128)(2,1)}, f32[1,256]{1,0:T(1,128)}) custom-call(bf16[128,1536]{1,0:T(8,128)(2,1)} %gradient.3, f32[128,1536]{1,0:T(8,128)} %momentum.3, bf16[256,1536]{1,0:T(8,128)(2,1)} %basis.1), custom_call_target="tpu_custom_call" | custom-call | tf_op jit(solution)/shard_map/pallas_call | solution.py:391
  86.5 3.2 %shard_map.68 = (bf16[128,1536]{1,0:T(8,128)(2,1)}, f32[128,1536]{1,0:T(8,128)}, bf16[256,1536]{1,0:T(8,128)(2,1)}) custom-call(bf16[128,1536]{1,0:T(8,128)(2,1)} %weight.1, bf16[128,1536]{1,0:T(8,128)(2,1)} %gradient.3, f32[128,1536]{1,0:T(8,128)} %momentum.3, bf16[128,256]{1,0:T(8,128)(2,1)} %get-tuple-element.6.ortho, ...), custom_call_target="tpu_custom_call" | custom-call | tf_op jit(solution)/shard_map/pallas_call | solution.py:441

commit v4 on v3

--- a/solution.py
+++ b/solution.py
@@ -108,7 +108,7 @@
     group = rows // 8
     for ob in range(size // rows):
         lo = ob * rows
-        if 2 * lo == size:
+        if 8 * lo == 3 * size:
             midway()
         panels = tuple(work[lo + 8 * i : lo + 8 * i + 8, :] for i in range(group))
         panels = lax.fori_loop(0, group, lambda t, ps: panel_step(t, ps, group), panels)

time: 89.9 us -> 89.7 us (level)
  no operation moved by 1% of the time
where the time goes in v4:
time: 89.7 us; the launch traced here: 89.5 us
  Pallas kernels  88.8 us (99%)
    pallas_call x1, Pallas kernels, per_device(): pl.pallas_call(functools.partial(exchange_kernel, sizes), out_shape=(jax....  85.7 us
    pallas_call x1, Pallas kernels, per_device(): pl.pallas_call(functools.partial(finish_kernel, factor), grid=(steps,), o...  3.15 us

profile of v4, /device:TPU:1, one launch (start us, length us, event | category | flops | bytes accessed | tf_op | source)
XLA Modules:
  0.0 89.5 jit_solution(11928718043778147073)
XLA Ops:
  0.6 85.7 %shard_map.67 = (bf16[128,256]{1,0:T(8,128)(2,1)}, bf16[64,24,256]{2,1,0:T(8,128)(2,1)}, f32[1,256]{1,0:T(1,128)}) custom-call(bf16[128,1536]{1,0:T(8,128)(2,1)} %gradient.3, f32[128,1536]{1,0:T(8,128)} %momentum.3, bf16[256,1536]{1,0:T(8,128)(2,1)} %basis.1), custom_call_target="tpu_custom_call" | custom-call | tf_op jit(solution)/shard_map/pallas_call | solution.py:391
  86.3 3.2 %shard_map.68 = (bf16[128,1536]{1,0:T(8,128)(2,1)}, f32[128,1536]{1,0:T(8,128)}, bf16[256,1536]{1,0:T(8,128)(2,1)}) custom-call(bf16[128,1536]{1,0:T(8,128)(2,1)} %weight.1, bf16[128,1536]{1,0:T(8,128)(2,1)} %gradient.3, f32[128,1536]{1,0:T(8,128)} %momentum.3, bf16[128,256]{1,0:T(8,128)(2,1)} %get-tuple-element.6.ortho, ...), custom_call_target="tpu_custom_call" | custom-call | tf_op jit(solution)/shard_map/pallas_call | solution.py:441
